TPU v7x, 32 devices: a whole 2x2x4 slice. The times are simulated.
32 devices in a mesh: prow: 4 (over y, x), pcol: 8 (over z, core).
Axes of the slice: x: 2, y: 2, z: 4, core: 2. Of those that a mesh axis runs over, the one named last changes fastest.
Arguments:
- ancestor: float32 [12288, 12288], P('prow', 'pcol'), may hold values from -448 to 15360, as said below
- factor: bfloat16 [2, 12288, 256], P(None, 'prow'), may hold values from -0.0009765625 to 0.0009765625
- inverse_diag: bfloat16 [2, 256, 256], replicated, may hold values from -6 to 6
- block_mask: int32 [2, 48], replicated, may hold values 0 or 1
Outputs:
- column_block: float32 [2, 12288, 256], P(None, ('prow', 'pcol'))
- diagonal: float32 [2, 256, 256], replicated
Inputs may be any that keep to these rules, and one draw needn't show every extreme that they name: `ancestor`: symmetric.
All inputs are finite; a program needn't handle non-finite values.
Results may differ from a plain program's by a relative error of at most 0.0003.
Values may be sent and summed in bfloat16 or wider, within the bound.
A program may use at most 64 MiB of HBM per device.

v0:
```python
import jax
import jax.numpy as jnp
from jax import lax
from jax.experimental import pallas as pl
from jax.experimental.pallas import tpu as pltpu
from jax.sharding import PartitionSpec as P

WIDTH = 256


def split(x):
    high = lax.reduce_precision(x, 8, 7)
    low = x - high
    return high.astype(jnp.bfloat16), low.astype(jnp.bfloat16)


def dot(a, b):
    return jnp.dot(a, b, preferred_element_type=jnp.float32)


MESH = pl.DeviceIdType.MESH


def levels():
    n_rows = lax.axis_size("prow")
    n_deep = lax.axis_size("pcol") // 2
    row = lax.axis_index("prow")
    column = lax.axis_index("pcol")
    deep, core = lax.div(column, 2), lax.rem(column, 2)
    return (
        (2, core, lambda p: (row, deep * 2 + p)),
        (n_rows, row, lambda p: (p, column)),
        (n_deep, deep, lambda p: (row, p * 2 + core)),
    )


def part(ref, start, size):
    return ref.at[pl.ds(pl.multiple_of(start, 8), size)]


def sum_everywhere(term, acc, landed, gathered, sems, base, height, number):
    start = base
    size = height
    slot = base
    source = term
    sent = []
    starts = []
    for n, mine, device in levels():
        size = size // n
        copies = []
        for d in range(1, n):
            peer = lax.rem(mine + d, n)
            copy = pltpu.make_async_remote_copy(
                part(source, start + peer * size, size),
                landed.at[pl.ds(slot + (d - 1) * size, size)],
                sems.at[0, number],
                sems.at[1, number],
                device_id=device(peer),
                device_id_type=MESH,
            )
            copy.start()
            copies.append(copy)
            number += 1
        yield
        start = start + mine * size
        starts.append((start, size))
        total = part(source, start, size)[...]
        for d in range(1, n):
            copies[d - 1].wait_recv()
            total = total + landed[pl.ds(slot + (d - 1) * size, size)]
        slot += (n - 1) * size
        part(acc, start, size)[...] = total
        source = acc
        sent += copies
    part(gathered, start, size)[...] = total
    for (n, mine, device), (start, size) in reversed(list(zip(levels(), starts))):
        copies = []
        for d in range(1, n):
            peer = lax.rem(mine + d, n)
            copy = pltpu.make_async_remote_copy(
                part(gathered, start, size),
                part(gathered, start, size),
                sems.at[0, number],
                sems.at[1, number],
                device_id=device(peer),
                device_id_type=MESH,
            )
            copy.start()
            copies.append(copy)
            number += 1
        yield
        for copy in copies:
            copy.wait_recv()
        sent += copies
    for copy in sent:
        copy.wait_send()


def chunk_of(position, deep):
    across = lax.rem(position + deep, 2)
    along = lax.rem(lax.div(position, 2) + lax.div(deep, 2), 2)
    return 2 * lax.rem(across + along, 2) + along


def position_of(chunk, deep):
    along = lax.rem(chunk, 2)
    across = lax.rem(lax.div(chunk, 2) + along, 2)
    return lax.rem(across + deep, 2) + 2 * lax.rem(along + lax.div(deep, 2), 2)


LANES = 128


def remote(source, target, sems, piece, number, device):
    return pltpu.make_async_remote_copy(
        source,
        target,
        sems.at[0, piece, number],
        sems.at[1, piece, number],
        device_id=device,
        device_id_type=MESH,
    )


def fused_kernel(
    factor,
    mask,
    ancestor,
    out,
    gathered,
    turned,
    tiles,
    parts,
    first,
    second,
    sums,
    ended,
    landing,
    term,
    acc,
    landed,
    result,
    loads,
    sems,
    small_sems,
):
    n_rows = lax.axis_size("prow")
    n_cols = lax.axis_size("pcol")
    row = lax.axis_index("prow")
    column = lax.axis_index("pcol")
    count, rows_here, width = factor.shape
    slab = out.shape[1]
    pieces = slab // LANES
    half = count * width // 2
    flip_x = row + 1 - 2 * lax.rem(row, 2)
    flip_y = lax.rem(row + 2, 4)
    flip_both = 3 - row
    x_peer, y_peer = (flip_x, column), (flip_y, column)
    deep = lax.div(column, 2)
    place = column * n_rows + chunk_of(row, deep)
    target = (lax.div(place, n_cols), lax.rem(place, n_cols))
    here = row * n_cols + column
    from_column = lax.div(here, n_rows)
    origin = (position_of(lax.rem(here, n_rows), lax.div(from_column, 2)), from_column)
    order = (flip_both, flip_x, flip_y, row)
    buffers = tiles.shape[0]
    upper, lower = pl.ds(0, half), pl.ds(half, half)

    def load(t):
        start = pl.multiple_of(chunk_of(order[t % 4], deep) * slab + (t // 4) * LANES, LANES)
        return pltpu.make_async_copy(ancestor.at[:, pl.ds(start, LANES)], tiles.at[t % buffers], loads.at[t])

    for t in range(buffers):
        load(t).start()

    barrier = pltpu.get_barrier_semaphore()
    peers = [device(lax.rem(mine + d, n)) for n, mine, device in levels() for d in range(1, n)]
    for peer in peers:
        pl.semaphore_signal(barrier, inc=1, device_id=peer, device_id_type=MESH)

    @pl.when(place != here)
    def _():
        pl.semaphore_signal(barrier, inc=1, device_id=origin, device_id_type=MESH)

    for k in range(count):
        for i in range(0, rows_here, WIDTH):
            block = factor[k, pl.ds(i, WIDTH)].T.astype(jnp.float32) * mask[pl.ds(k, 1), pl.ds(i, WIDTH)]
            turned[pl.ds(k * width, width), pl.ds(i, WIDTH)] = block.astype(jnp.bfloat16)

    @pl.when(place != here)
    def _():
        pl.semaphore_wait(barrier, len(peers) + 1)

    @pl.when(place == here)
    def _():
        pl.semaphore_wait(barrier, len(peers))

    def early(j):
        return (
            remote(parts.at[4 * j, upper], first.at[j, 0], sems, j, 0, x_peer),
            remote(parts.at[4 * j + 1, upper], first.at[j, 1], sems, j, 1, x_peer),
            remote(parts.at[4 * j, lower], first.at[j, 2], sems, j, 2, y_peer),
            remote(parts.at[4 * j + 2, lower], first.at[j, 3], sems, j, 3, y_peer),
        )

    def late(j):
        return (
            remote(sums.at[j, 0], second.at[j, 0], sems, j, 4, y_peer),
            remote(sums.at[j, 1], second.at[j, 1], sems, j, 5, x_peer),
        )

    def final(j):
        return remote(ended.at[j], landing.at[j], sems, j, 6, target)

    def compute(j):
        for q in range(4):
            t = 4 * j + q
            load(t).wait()
            value = tiles[t % buffers]
            high = value.astype(jnp.bfloat16)
            low = (value - high.astype(jnp.float32)).astype(jnp.bfloat16)
            both = dot(turned[...], jnp.concatenate([high, low], axis=1))
            parts[t] = both[:, :LANES] + both[:, LANES:]
            if t + buffers < 4 * pieces:
                load(t + buffers).start()
            copies = early(j)
            for i in ((0, 2), (1,), (3,), ())[q]:
                copies[i].start()

    def forward(j):
        copies = early(j)
        copies[0].wait_recv()
        sums[j, 0] = parts[4 * j + 2, upper] + first[j, 0]
        late(j)[0].start()
        copies[2].wait_recv()
        sums[j, 1] = parts[4 * j + 1, lower] + first[j, 2]
        late(j)[1].start()

    def end(j):
        copies = early(j)
        copies[1].wait_recv()
        copies[3].wait_recv()
        late(j)[0].wait_recv()
        late(j)[1].wait_recv()
        ended[j, upper] = parts[4 * j + 3, upper] + first[j, 1] + second[j, 0]
        ended[j, lower] = parts[4 * j + 3, lower] + first[j, 3] + second[j, 1]

        @pl.when(place != here)
        def _():
            final(j).start()

        @pl.when(place == here)
        def _():
            landing[j] = ended[j]

    for j in range(pieces):
        compute(j)
        if j >= 1:
            forward(j - 1)
        if j >= 2:
            end(j - 2)
    forward(pieces - 1)
    for j in range(max(pieces - 2, 0), pieces):
        end(j)
    totals = [0.0] * count
    for j in range(pieces):
        @pl.when(place != here)
        def _():
            final(j).wait_recv()

        lanes = pl.ds(pl.multiple_of(column * slab + j * LANES, LANES), LANES)
        for k in range(count):
            rows = pl.ds(k * width, width)
            value = landing[j, rows]
            high = value.astype(jnp.bfloat16)
            low = (value - high.astype(jnp.float32)).astype(jnp.bfloat16)
            own = turned[rows, lanes]
            totals[k] = totals[k] + lax.dot_general(
                jnp.concatenate([own, own], axis=1),
                jnp.concatenate([high, low], axis=1),
                (((1,), (1,)), ((), ())),
                preferred_element_type=jnp.float32,
            )
    for k in range(count):
        term[pl.ds(k * width, width)] = totals[k]

    def meanwhile():
        for j in range(pieces):
            for k in range(count):
                out[k, pl.ds(j * LANES, LANES)] = landing[j, pl.ds(k * width, width)].T

    each = small_sems.shape[1] // 2
    halves = [
        sum_everywhere(term, acc, landed, result, small_sems, h * half, half, h * each) for h in range(2)
    ]
    for depth in range(7):
        for running in halves:
            next(running, None)
        if depth == 1:
            meanwhile()
    gathered[...] = result[...]
    for j in range(pieces):
        @pl.when(place != here)
        def _():
            final(j).wait_send()

        for copy in early(j) + late(j):
            copy.wait_send()


def fused(factor, mask, ancestor):
    count, depth, width = factor.shape
    height = count * width
    n_rows, n_cols = lax.axis_size("prow"), lax.axis_size("pcol")
    slab = ancestor.shape[1] // n_rows
    pieces = slab // LANES
    half = height // 2
    vmem = pl.BlockSpec(memory_space=pltpu.VMEM)
    f32 = jnp.float32
    block = pltpu.VMEM((height, width), f32)
    small = 4 * (1 + n_rows - 1 + n_cols // 2 - 1)
    return pl.pallas_call(
        fused_kernel,
        out_shape=(
            jax.ShapeDtypeStruct((count, slab, width), f32),
            jax.ShapeDtypeStruct((height, width), f32),
        ),
        in_specs=[vmem, vmem, pl.BlockSpec(memory_space=pl.ANY)],
        out_specs=(vmem, vmem),
        scratch_shapes=[
            pltpu.VMEM((height, depth), jnp.bfloat16),
            pltpu.VMEM((4, depth, LANES), f32),
            pltpu.VMEM((4 * pieces, height, LANES), f32),
            pltpu.VMEM((pieces, 4, half, LANES), f32),
            pltpu.VMEM((pieces, 2, half, LANES), f32),
            pltpu.VMEM((pieces, 2, half, LANES), f32),
            pltpu.VMEM((pieces, height, LANES), f32),
            pltpu.VMEM((pieces, height, LANES), f32),
            block,
            block,
            block,
            block,
            pltpu.SemaphoreType.DMA((4 * pieces,)),
            pltpu.SemaphoreType.DMA((2, pieces, 7)),
            pltpu.SemaphoreType.DMA((2, small)),
        ],
        compiler_params=pltpu.CompilerParams(
            collective_id=1, has_side_effects=True, vmem_limit_bytes=48 * 1024 * 1024
        ),
    )(factor, mask, ancestor)


def product_plain(turned, ancestor):
    n_rows = lax.axis_size("prow")
    n_cols = lax.axis_size("pcol")
    high, low = split(ancestor)
    partial = dot(turned, high) + dot(turned, low)
    summed = lax.psum_scatter(partial, "prow", scatter_dimension=1, tiled=True)
    pairs = [(r * n_cols + c, c * n_rows + r) for r in range(n_rows) for c in range(n_cols)]
    return lax.ppermute(summed, ("prow", "pcol"), pairs)


def shards(ancestor, factor, inverse_diag, block_mask):
    rows_here = ancestor.shape[0]
    count, _, width = factor.shape
    n_rows = lax.axis_size("prow")
    n_cols = lax.axis_size("pcol")
    column = lax.axis_index("pcol")
    grid_row = lax.axis_index("prow")
    slab = rows_here // n_cols
    row_mask = jnp.repeat(block_mask, WIDTH, axis=1).astype(jnp.float32)
    own_mask = lax.dynamic_slice_in_dim(row_mask, grid_row * rows_here, rows_here, 1)
    slab_mask = lax.dynamic_slice_in_dim(own_mask, column * slab, slab, 1)
    inverse = inverse_diag.astype(jnp.float32)
    fits = n_rows == 4 and n_cols % 2 == 0 and count % 2 == 0
    fits = fits and slab % LANES == 0 and count * width % (16 * n_rows * n_cols) == 0
    if fits:
        placed, total = fused(factor, own_mask, ancestor)
        return (-slab_mask[:, :, None] * placed, inverse + total.reshape(inverse.shape))
    masked = factor * own_mask[:, :, None].astype(factor.dtype)
    turned = masked.transpose(0, 2, 1).reshape(count * width, rows_here)
    placed = product_plain(turned, ancestor).reshape(count, width, slab)
    column_block = -slab_mask[:, :, None] * placed.transpose(0, 2, 1)
    own_slab = lax.dynamic_slice_in_dim(masked, column * slab, slab, 1)
    high, low = split(column_block)
    term = jnp.stack([dot(own_slab[k].T, high[k]) + dot(own_slab[k].T, low[k]) for k in range(count)])
    return (column_block, inverse - lax.psum(term, ("prow", "pcol")))


def solution(mesh):
    return jax.shard_map(
        shards,
        mesh=mesh,
        in_specs=(P("prow", "pcol"), P(None, "prow", None), P(), P()),
        out_specs=(P(None, ("prow", "pcol"), None), P()),
        check_vma=False,
    )
```

profile of v0, /device:TPU:0, one launch (start us, length us, event | category | flops | bytes accessed | tf_op | source)
XLA Modules:
  0.0 76.7 jit_solution(16540097460078234389)
XLA Ops:
  0.6 0.0 copy-start.1
  0.7 0.7 convert_element_type.10
  1.4 0.1 broadcast_bitcast_fusion
  1.5 0.1 copy.6
  1.5 0.1 dynamic-slice_negate_fusion
  1.6 0.0 copy-start
  1.6 1.9 %copy-done = bf16[2,3072,256]{2,1,0:T(8,128)(2,1)S(1)} copy-done((bf16[2,3072,256]{2,1,0:T(8,128)(2,1)S(1)}, bf16[2,3072,256]{2,1,0:T(8,128)(2,1)}, u32[]{:S(2)}) %copy-start) | copy-done | bytes 3145752
  3.5 71.3 %shard_map.59 = (f32[2,384,256]{2,1,0:T(8,128)S(1)}, f32[512,256]{1,0:T(8,128)S(1)}) custom-call(bf16[2,3072,256]{2,1,0:T(8,128)(2,1)S(1)} %copy-done, f32[2,3072]{1,0:T(2,128)S(1)} %constant_dynamic-slice_fusion.mask, f32[3072,1536]{1,0:T(8,128)} %ancestor.1), custom_call_target="tpu_custom_call" | custom-call | tf_op jit(solution)/shard_map/pallas_call | solution.py:322
  74.8 1.0 %broadcast_multiply_fusion = f32[2,384,256]{2,1,0:T(8,128)} fusion(f32[2,384,256]{2,1,0:T(8,128)S(1)} %get-tuple-element.4, f32[2,384]{1,0:T(2,128)S(1)} %dynamic-slice_negate_fusion), kind=kLoop, calls=%fused_computation.1 | loop fusion | flops 196608 | bytes 1575936 | tf_op jit(solution)/shard_map/mul | solution.py:379
  75.8 0.0 copy-done.1
  75.8 0.9 %convert_add_fusion = f32[2,256,256]{2,1,0:T(8,128)} fusion(f32[2,256,256]{2,1,0:T(8,128)S(1)} %bitcast.4, bf16[2,256,256]{2,1,0:T(8,128)(2,1)S(1)} %copy-done.1), kind=kLoop, calls=%fused_computation | loop fusion | flops 262144 | bytes 1310720 | tf_op jit(solution)/shard_map/add | solution.py:379
  (1 shorter events, 0.0 us)
Async XLA Ops:
  0.6 75.2 %copy-start.1 = (bf16[2,256,256]{2,1,0:T(8,128)(2,1)S(1)}, bf16[2,256,256]{2,1,0:T(8,128)(2,1)}, u32[]{:S(2)}) copy-start(bf16[2,256,256]{2,1,0:T(8,128)(2,1)} %param.6) | copy-start | bytes 786436
  1.6 1.9 %copy-start = (bf16[2,3072,256]{2,1,0:T(8,128)(2,1)S(1)}, bf16[2,3072,256]{2,1,0:T(8,128)(2,1)}, u32[]{:S(2)}) copy-start(bf16[2,3072,256]{2,1,0:T(8,128)(2,1)} %factor.1) | copy-start | bytes 9437188
where the time goes:
time: 76.9 us; the launch traced here: 76.7 us
  Pallas kernels  71.3 us (93%)
  other arithmetic  2.71 us (4%)
  local copies, waits for them, and re-layouts  2.05 us (3%)
    pallas_call x1, Pallas kernels, fused(): pl.pallas_call(fused_kernel, out_shape=(jax.ShapeDtypeStruct((count, slab...  71.3 us
    unnamed x6, local copies, waits for them, and re-layouts  2.05 us

commit v1 on v0

v1 whole, which is shorter than its diff:
```python
import jax
import jax.numpy as jnp
from jax import lax
from jax.experimental import pallas as pl
from jax.experimental.pallas import tpu as pltpu
from jax.sharding import PartitionSpec as P

WIDTH = 256


def split(x):
    high = lax.reduce_precision(x, 8, 7)
    low = x - high
    return high.astype(jnp.bfloat16), low.astype(jnp.bfloat16)


def dot(a, b):
    return jnp.dot(a, b, preferred_element_type=jnp.float32)


MESH = pl.DeviceIdType.MESH


STEPS = 32.0
BIAS = 4096.0
REACH = 32760.0
HEAD = 16


def part(ref, start, size):
    return ref.at[pl.ds(pl.multiple_of(start, 8), size)]


def encode(value, wire):
    top = jnp.max(jnp.abs(value), axis=0, keepdims=True)
    code = jnp.ceil(jnp.log2(jnp.maximum(top, 1e-30)) * STEPS) + 1.0
    scale = jnp.exp2(code * (-1.0 / STEPS)) * REACH
    number = (code + BIAS).astype(jnp.int32)
    place = lax.broadcasted_iota(jnp.int32, (HEAD, value.shape[1]), 0)
    bits = lax.shift_right_logical(jnp.broadcast_to(number, place.shape), place) & 1
    head = jnp.round(value[:HEAD] * (scale * 0.5)).astype(jnp.int32) * 2 + bits
    rest = jnp.round(value[HEAD:] * scale).astype(jnp.int32)
    wire[...] = jnp.concatenate([head, rest], axis=0).astype(jnp.int16)


def decode(wire):
    value = wire[...].astype(jnp.int32)
    head = value[:HEAD]
    bits = head & 1
    place = lax.broadcasted_iota(jnp.int32, head.shape, 0)
    number = jnp.sum(lax.shift_left(bits, place).astype(jnp.float32), axis=0, keepdims=True)
    scale = jnp.exp2((number - BIAS) * (1.0 / STEPS)) * (1.0 / REACH)
    return jnp.concatenate([head - bits, value[HEAD:]], axis=0).astype(jnp.float32) * scale


def chunk_of(position, deep):
    across = lax.rem(position + deep, 2)
    along = lax.rem(lax.div(position, 2) + lax.div(deep, 2), 2)
    return 2 * lax.rem(across + along, 2) + along


def position_of(chunk, deep):
    along = lax.rem(chunk, 2)
    across = lax.rem(lax.div(chunk, 2) + along, 2)
    return lax.rem(across + deep, 2) + 2 * lax.rem(along + lax.div(deep, 2), 2)


LANES = 128


def remote(source, target, sems, piece, number, device):
    return pltpu.make_async_remote_copy(
        source,
        target,
        sems.at[0, piece, number],
        sems.at[1, piece, number],
        device_id=device,
        device_id_type=MESH,
    )


def fused_kernel(
    factor,
    mask,
    ancestor,
    out,
    gathered,
    turned,
    tiles,
    parts,
    first_out,
    first,
    second_out,
    second,
    ended,
    landing,
    term,
    plane_out,
    plane,
    line,
    shared,
    loads,
    sems,
    plane_sems,
    line_sems,
    shared_sems,
):
    n_rows = lax.axis_size("prow")
    n_cols = lax.axis_size("pcol")
    n_deep = n_cols // 2
    row = lax.axis_index("prow")
    column = lax.axis_index("pcol")
    count, rows_here, width = factor.shape
    slab = out.shape[1]
    lanes_each = slab // LANES
    pieces = count * lanes_each
    half = width // 2
    flip_x = row + 1 - 2 * lax.rem(row, 2)
    flip_y = lax.rem(row + 2, 4)
    flip_both = 3 - row
    x_peer, y_peer = (flip_x, column), (flip_y, column)
    deep, core = lax.div(column, 2), lax.rem(column, 2)
    place = column * n_rows + chunk_of(row, deep)
    target = (lax.div(place, n_cols), lax.rem(place, n_cols))
    here = row * n_cols + column
    from_column = lax.div(here, n_rows)
    origin = (position_of(lax.rem(here, n_rows), lax.div(from_column, 2)), from_column)
    order = (flip_both, flip_x, flip_y, row)
    upper, lower = pl.ds(0, half), pl.ds(half, half)
    group = 2 * n_rows
    member = row * 2 + core
    height = width // group

    def load(t):
        start = pl.multiple_of(chunk_of(order[t % 4], deep) * slab + (t // 4) * LANES, LANES)
        return pltpu.make_async_copy(ancestor.at[:, pl.ds(start, LANES)], tiles.at[t], loads.at[t])

    for t in range(4 * lanes_each):
        load(t).start()

    def in_plane(d):
        peer = lax.rem(member + d, group)
        return peer, (lax.div(peer, 2), deep * 2 + lax.rem(peer, 2))

    def on_line(d):
        peer = lax.rem(deep + d, n_deep)
        return (row, peer * 2 + core)

    barrier = pltpu.get_barrier_semaphore()
    peers = [in_plane(d)[1] for d in range(1, group)] + [on_line(d) for d in range(1, n_deep)]
    for peer in peers:
        pl.semaphore_signal(barrier, inc=1, device_id=peer, device_id_type=MESH)

    @pl.when(place != here)
    def _():
        pl.semaphore_signal(barrier, inc=1, device_id=origin, device_id_type=MESH)

    def turn(k):
        for i in range(0, rows_here, WIDTH):
            block = factor[k, pl.ds(i, WIDTH)].T.astype(jnp.float32) * mask[pl.ds(k, 1), pl.ds(i, WIDTH)]
            turned[pl.ds(k * width, width), pl.ds(i, WIDTH)] = block.astype(jnp.bfloat16)

    turn(0)

    @pl.when(place != here)
    def _():
        pl.semaphore_wait(barrier, len(peers) + 1)

    @pl.when(place == here)
    def _():
        pl.semaphore_wait(barrier, len(peers))

    def early(i, s):
        return remote(first_out.at[i, s], first.at[i, s], sems, i, s, (x_peer, x_peer, y_peer, y_peer)[s])

    def late(i, s):
        return remote(second_out.at[i, s], second.at[i, s], sems, i, 4 + s, (y_peer, x_peer)[s])

    def final(i):
        return remote(ended.at[i], landing.at[i], sems, i, 6, target)

    def compute(i):
        k, j = divmod(i, lanes_each)
        for q in range(4):
            t = 4 * j + q
            if k == 0:
                load(t).wait()
            value = tiles[t]
            high = value.astype(jnp.bfloat16)
            low = (value - high.astype(jnp.float32)).astype(jnp.bfloat16)
            both = dot(turned[pl.ds(k * width, width)], jnp.concatenate([high, low], axis=1))
            parts[4 * i + q] = both[:, :LANES] + both[:, LANES:]
            for s in ((0, 2), (1,), (3,), ())[q]:
                encode(parts[4 * i + q, (upper, upper, lower, lower)[s]], first_out.at[i, s])
                early(i, s).start()

    def forward(i):
        early(i, 0).wait_recv()
        encode(parts[4 * i + 2, upper] + decode(first.at[i, 0]), second_out.at[i, 0])
        late(i, 0).start()
        early(i, 2).wait_recv()
        encode(parts[4 * i + 1, lower] + decode(first.at[i, 2]), second_out.at[i, 1])
        late(i, 1).start()

    def end(i):
        early(i, 1).wait_recv()
        early(i, 3).wait_recv()
        late(i, 0).wait_recv()
        late(i, 1).wait_recv()
        ready = parts[4 * i + 3, upper] + decode(first.at[i, 1]) + decode(second.at[i, 0])
        encode(ready, ended.at[i, upper])
        ready = parts[4 * i + 3, lower] + decode(first.at[i, 3]) + decode(second.at[i, 1])
        encode(ready, ended.at[i, lower])

        @pl.when(place != here)
        def _():
            final(i).start()

        @pl.when(place == here)
        def _():
            landing[i] = ended[i]

    def diagonal(k):
        total = 0.0
        for j in range(lanes_each):
            i = k * lanes_each + j

            @pl.when(place != here)
            def _():
                final(i).wait_recv()

            value = jnp.concatenate([decode(landing.at[i, upper]), decode(landing.at[i, lower])], axis=0)
            parts[4 * i] = value
            high = value.astype(jnp.bfloat16)
            low = (value - high.astype(jnp.float32)).astype(jnp.bfloat16)
            lanes = pl.ds(pl.multiple_of(column * slab + j * LANES, LANES), LANES)
            own = turned[pl.ds(k * width, width), lanes]
            total = total + lax.dot_general(
                jnp.concatenate([own, own], axis=1),
                jnp.concatenate([high, low], axis=1),
                (((1,), (1,)), ((), ())),
                preferred_element_type=jnp.float32,
            )
        term[k] = total
        copies = []
        for d in range(1, group):
            peer, device = in_plane(d)
            encode(term[k, pl.ds(pl.multiple_of(peer * height, height), height)], plane_out.at[k, d - 1])
            copy = remote(plane_out.at[k, d - 1], plane.at[k, d - 1], plane_sems, k, d - 1, device)
            copy.start()
            copies.append(copy)
        yield
        total = term[k, pl.ds(pl.multiple_of(member * height, height), height)]
        for d in range(1, group):
            copies[d - 1].wait_recv()
            total = total + decode(plane.at[k, d - 1])
        encode(total, line.at[k, deep])
        sent = copies
        copies = []
        for d in range(1, n_deep):
            copy = remote(line.at[k, deep], line.at[k, deep], line_sems, k, d - 1, on_line(d))
            copy.start()
            copies.append(copy)
        yield
        for copy in copies:
            copy.wait_recv()
        total = decode(line.at[k, 0])
        for d in range(1, n_deep):
            total = total + decode(line.at[k, d])
        encode(total, shared.at[k, member])
        sent = sent + copies
        copies = []
        for d in range(1, group):
            copy = remote(
                shared.at[k, member], shared.at[k, member], shared_sems, k, d - 1, in_plane(d)[1]
            )
            copy.start()
            copies.append(copy)
        yield
        for copy in copies:
            copy.wait_recv()
        for d in range(group):
            gathered[pl.ds(k * width + d * height, height)] = decode(shared.at[k, d])
        for copy in sent + copies:
            copy.wait_send()

    def turn_back(k):
        for j in range(lanes_each):
            out[k, pl.ds(j * LANES, LANES)] = parts[4 * (k * lanes_each + j)].T

    compute(0)
    for k in range(1, count):
        turn(k)
    for i in range(1, pieces):
        compute(i)
        forward(i - 1)
        if i >= 2:
            end(i - 2)
    forward(pieces - 1)
    running = [diagonal(k) for k in range(count)]
    for k in range(count - 1):
        next(running[k])
    end(pieces - 2)
    for k in range(count - 1):
        next(running[k])
    end(pieces - 1)
    for k in range(count - 1):
        next(running[k])
        turn_back(k)
    next(running[count - 1])
    turn_back(count - 1)
    for _ in range(2):
        next(running[count - 1])
    for k in range(count):
        next(running[k], None)
    for i in range(pieces):
        @pl.when(place != here)
        def _():
            final(i).wait_send()

        for s in range(4):
            early(i, s).wait_send()
        for s in range(2):
            late(i, s).wait_send()


def fused(factor, mask, ancestor):
    count, depth, width = factor.shape
    n_rows, n_cols = lax.axis_size("prow"), lax.axis_size("pcol")
    slab = ancestor.shape[1] // n_rows
    lanes_each = slab // LANES
    pieces = count * lanes_each
    half = width // 2
    group, n_deep = 2 * n_rows, n_cols // 2
    height = width // group
    vmem = pl.BlockSpec(memory_space=pltpu.VMEM)
    f32, i16 = jnp.float32, jnp.int16
    return pl.pallas_call(
        fused_kernel,
        out_shape=(
            jax.ShapeDtypeStruct((count, slab, width), f32),
            jax.ShapeDtypeStruct((count * width, width), f32),
        ),
        in_specs=[vmem, vmem, pl.BlockSpec(memory_space=pl.ANY)],
        out_specs=(vmem, vmem),
        scratch_shapes=[
            pltpu.VMEM((count * width, depth), jnp.bfloat16),
            pltpu.VMEM((4 * lanes_each, depth, LANES), f32),
            pltpu.VMEM((4 * pieces, width, LANES), f32),
            pltpu.VMEM((pieces, 4, half, LANES), i16),
            pltpu.VMEM((pieces, 4, half, LANES), i16),
            pltpu.VMEM((pieces, 2, half, LANES), i16),
            pltpu.VMEM((pieces, 2, half, LANES), i16),
            pltpu.VMEM((pieces, width, LANES), i16),
            pltpu.VMEM((pieces, width, LANES), i16),
            pltpu.VMEM((count, width, width), f32),
            pltpu.VMEM((count, group - 1, height, width), i16),
            pltpu.VMEM((count, group - 1, height, width), i16),
            pltpu.VMEM((count, n_deep, height, width), i16),
            pltpu.VMEM((count, group, height, width), i16),
            pltpu.SemaphoreType.DMA((4 * lanes_each,)),
            pltpu.SemaphoreType.DMA((2, pieces, 7)),
            pltpu.SemaphoreType.DMA((2, count, group - 1)),
            pltpu.SemaphoreType.DMA((2, count, n_deep - 1)),
            pltpu.SemaphoreType.DMA((2, count, group - 1)),
        ],
        compiler_params=pltpu.CompilerParams(
            collective_id=1, has_side_effects=True, vmem_limit_bytes=56 * 1024 * 1024
        ),
    )(factor, mask, ancestor)


def product_plain(turned, ancestor):
    n_rows = lax.axis_size("prow")
    n_cols = lax.axis_size("pcol")
    high, low = split(ancestor)
    partial = dot(turned, high) + dot(turned, low)
    summed = lax.psum_scatter(partial, "prow", scatter_dimension=1, tiled=True)
    pairs = [(r * n_cols + c, c * n_rows + r) for r in range(n_rows) for c in range(n_cols)]
    return lax.ppermute(summed, ("prow", "pcol"), pairs)


def shards(ancestor, factor, inverse_diag, block_mask):
    rows_here = ancestor.shape[0]
    count, _, width = factor.shape
    n_rows = lax.axis_size("prow")
    n_cols = lax.axis_size("pcol")
    column = lax.axis_index("pcol")
    grid_row = lax.axis_index("prow")
    slab = rows_here // n_cols
    row_mask = jnp.repeat(block_mask, WIDTH, axis=1).astype(jnp.float32)
    own_mask = lax.dynamic_slice_in_dim(row_mask, grid_row * rows_here, rows_here, 1)
    slab_mask = lax.dynamic_slice_in_dim(own_mask, column * slab, slab, 1)
    inverse = inverse_diag.astype(jnp.float32)
    fits = n_rows == 4 and n_cols % 2 == 0 and n_cols > 2 and width == WIDTH
    fits = fits and slab % LANES == 0 and slab * n_rows == ancestor.shape[1]
    if fits:
        placed, total = fused(factor, own_mask, ancestor)
        return (-slab_mask[:, :, None] * placed, inverse + total.reshape(inverse.shape))
    masked = factor * own_mask[:, :, None].astype(factor.dtype)
    turned = masked.transpose(0, 2, 1).reshape(count * width, rows_here)
    placed = product_plain(turned, ancestor).reshape(count, width, slab)
    column_block = -slab_mask[:, :, None] * placed.transpose(0, 2, 1)
    own_slab = lax.dynamic_slice_in_dim(masked, column * slab, slab, 1)
    high, low = split(column_block)
    term = jnp.stack([dot(own_slab[k].T, high[k]) + dot(own_slab[k].T, low[k]) for k in range(count)])
    return (column_block, inverse - lax.psum(term, ("prow", "pcol")))


def solution(mesh):
    return jax.shard_map(
        shards,
        mesh=mesh,
        in_specs=(P("prow", "pcol"), P(None, "prow", None), P(), P()),
        out_specs=(P(None, ("prow", "pcol"), None), P()),
        check_vma=False,
    )
```

time: 76.9 us -> 64 us (0.83)
  Pallas kernels: 71.3 us -> 57.4 us
  other arithmetic: 2.71 us -> 4.87 us
  local copies, waits for them, and re-layouts: 2.05 us -> 0.77 us
    pallas_call x1, Pallas kernels: 71.3 us -> 57.4 us  [fused(): pl.pallas_call(fused_kernel, out_shape=(jax.ShapeDtypeStruct((count, slab...]
    unnamed x6 -> x4, local copies, waits for them, and re-layouts: 2.05 us -> 0.16 us
    mul x1, other arithmetic: 1.05 us -> 2.18 us  [shards(): -slab_mask[:, :, None] * placed]
    add x1, other arithmetic: 0.86 us -> 1.89 us  [shards(): inverse + total.reshape(inverse.shape)]
where the time goes in v1:
time: 64 us; the launch traced here: 63.7 us
  Pallas kernels  57.4 us (90%)
  other arithmetic  4.87 us (8%)
  local copies, waits for them, and re-layouts  0.77 us (1%)
  between operations  0.67 us (1%)
    pallas_call x1, Pallas kernels, fused(): pl.pallas_call(fused_kernel, out_shape=(jax.ShapeDtypeStruct((count, slab...  57.4 us
    mul x1, other arithmetic, shards(): -slab_mask[:, :, None] * placed  2.18 us
    add x1, other arithmetic, shards(): inverse + total.reshape(inverse.shape)  1.89 us

profile of v1, /device:TPU:0, one launch (start us, length us, event | category | flops | bytes accessed | tf_op | source)
XLA Modules:
  0.0 63.7 jit_solution(3187119002975411403)
XLA Ops:
  0.6 0.0 copy-start
  0.7 0.7 %convert_element_type.10 = f32[2,48]{1,0:T(2,128)S(1)} convert(s32[2,48]{1,0:T(2,128)} %param.7) | non-fusion elementwise | flops 96 | bytes 768 | tf_op jit(solution)/shard_map/convert_element_type | solution.py:391
  1.4 0.1 broadcast_bitcast_fusion
  1.5 0.1 copy.6
  1.5 0.1 dynamic-slice_negate_fusion
  1.6 0.6 constant_dynamic-slice_fusion.mask
  2.2 57.4 %shard_map.59 = (f32[2,384,256]{2,1,0:T(8,128)}, f32[512,256]{1,0:T(8,128)}) custom-call(bf16[2,3072,256]{2,1,0:T(8,128)(2,1)} %factor.1, f32[2,3072]{1,0:T(2,128)} %constant_dynamic-slice_fusion.mask, f32[3072,1536]{1,0:T(8,128)} %ancestor.1), custom_call_target="tpu_custom_call" | custom-call | tf_op jit(solution)/shard_map/pallas_call | solution.py:338
  59.7 2.2 %broadcast_multiply_fusion = f32[2,384,256]{2,1,0:T(8,128)} fusion(f32[2,384,256]{2,1,0:T(8,128)} %get-tuple-element.4, f32[2,384]{1,0:T(2,128)S(1)} %dynamic-slice_negate_fusion), kind=kLoop, calls=%fused_computation.1 | loop fusion | flops 196608 | bytes 1575936 | tf_op jit(solution)/shard_map/mul | solution.py:399
  61.8 0.0 copy-done
  61.8 1.9 %convert_add_fusion = f32[2,256,256]{2,1,0:T(8,128)} fusion(f32[2,256,256]{2,1,0:T(8,128)} %bitcast.4, bf16[2,256,256]{2,1,0:T(8,128)(2,1)S(1)} %copy-done), kind=kLoop, calls=%fused_computation | loop fusion | flops 262144 | bytes 1310720 | tf_op jit(solution)/shard_map/add | solution.py:399
Async XLA Ops:
  0.6 61.2 %copy-start = (bf16[2,256,256]{2,1,0:T(8,128)(2,1)S(1)}, bf16[2,256,256]{2,1,0:T(8,128)(2,1)}, u32[]{:S(2)}) copy-start(bf16[2,256,256]{2,1,0:T(8,128)(2,1)} %param.6) | copy-start | bytes 786436

commit v2 on v1

--- a/solution.py
+++ b/solution.py
@@ -188,8 +188,10 @@
             value = tiles[t]
             high = value.astype(jnp.bfloat16)
             low = (value - high.astype(jnp.float32)).astype(jnp.bfloat16)
-            both = dot(turned[pl.ds(k * width, width)], jnp.concatenate([high, low], axis=1))
-            parts[4 * i + q] = both[:, :LANES] + both[:, LANES:]
+            stacked = jnp.concatenate([high, low], axis=1)
+            for h in range(2):
+                both = dot(turned[pl.ds(k * width + h * half, half)], stacked)
+                parts[4 * i + q, pl.ds(h * half, half)] = both[:, :LANES] + both[:, LANES:]
             for s in ((0, 2), (1,), (3,), ())[q]:
                 encode(parts[4 * i + q, (upper, upper, lower, lower)[s]], first_out.at[i, s])
                 early(i, s).start()

time: 64 us -> 57.5 us (0.90)
  Pallas kernels: 57.4 us -> 51 us
    pallas_call x1, Pallas kernels: 57.4 us -> 51 us  [fused(): pl.pallas_call(fused_kernel, out_shape=(jax.ShapeDtypeStruct((count, slab...]
where the time goes in v2:
time: 57.5 us; the launch traced here: 57.3 us
  Pallas kernels  51 us (89%)
  other arithmetic  4.87 us (8%)
  local copies, waits for them, and re-layouts  0.77 us (1%)
  between operations  0.67 us (1%)
    pallas_call x1, Pallas kernels, fused(): pl.pallas_call(fused_kernel, out_shape=(jax.ShapeDtypeStruct((count, slab...  51 us
    mul x1, other arithmetic, shards(): -slab_mask[:, :, None] * placed  2.18 us
    add x1, other arithmetic, shards(): inverse + total.reshape(inverse.shape)  1.89 us

profile of v2, /device:TPU:0, one launch (start us, length us, event | category | flops | bytes accessed | tf_op | source)
XLA Modules:
  0.0 57.3 jit_solution(8786426803989001900)
XLA Ops:
  0.6 0.0 copy-start
  0.7 0.7 %convert_element_type.10 = f32[2,48]{1,0:T(2,128)S(1)} convert(s32[2,48]{1,0:T(2,128)} %param.7) | non-fusion elementwise | flops 96 | bytes 768 | tf_op jit(solution)/shard_map/convert_element_type | solution.py:393
  1.4 0.1 broadcast_bitcast_fusion
  1.5 0.1 copy.6
  1.5 0.1 dynamic-slice_negate_fusion
  1.6 0.6 %constant_dynamic-slice_fusion.mask = f32[2,3072]{1,0:T(2,128)} fusion(f32[2,12288]{1,0:T(2,128)S(1)} %bitcast.6, s32[]{:T(128)S(6)} %select_n.12), kind=kLoop, calls=%fused_computation.4 | loop fusion | bytes 49156 | tf_op jit(solution)/shard_map/dynamic_slice | solution.py:394
  2.2 51.0 %shard_map.59 = (f32[2,384,256]{2,1,0:T(8,128)}, f32[512,256]{1,0:T(8,128)}) custom-call(bf16[2,3072,256]{2,1,0:T(8,128)(2,1)} %factor.1, f32[2,3072]{1,0:T(2,128)} %constant_dynamic-slice_fusion.mask, f32[3072,1536]{1,0:T(8,128)} %ancestor.1), custom_call_target="tpu_custom_call" | custom-call | tf_op jit(solution)/shard_map/pallas_call | solution.py:340
  53.2 2.2 %broadcast_multiply_fusion = f32[2,384,256]{2,1,0:T(8,128)} fusion(f32[2,384,256]{2,1,0:T(8,128)} %get-tuple-element.4, f32[2,384]{1,0:T(2,128)S(1)} %dynamic-slice_negate_fusion), kind=kLoop, calls=%fused_computation.1 | loop fusion | flops 196608 | bytes 1575936 | tf_op jit(solution)/shard_map/mul | solution.py:401
  55.4 0.0 copy-done
  55.4 1.9 %convert_add_fusion = f32[2,256,256]{2,1,0:T(8,128)} fusion(f32[2,256,256]{2,1,0:T(8,128)} %bitcast.4, bf16[2,256,256]{2,1,0:T(8,128)(2,1)S(1)} %copy-done), kind=kLoop, calls=%fused_computation | loop fusion | flops 262144 | bytes 1310720 | tf_op jit(solution)/shard_map/add | solution.py:401
Async XLA Ops:
  0.6 54.8 %copy-start = (bf16[2,256,256]{2,1,0:T(8,128)(2,1)S(1)}, bf16[2,256,256]{2,1,0:T(8,128)(2,1)}, u32[]{:S(2)}) copy-start(bf16[2,256,256]{2,1,0:T(8,128)(2,1)} %param.6) | copy-start | bytes 786436

commit v3 on v2

--- a/solution.py
+++ b/solution.py
@@ -66,6 +66,7 @@
 
 
 LANES = 128
+AHEAD = 3
 
 
 def remote(source, target, sems, piece, number, device):
@@ -80,11 +81,12 @@
 
 
 def fused_kernel(
-    factor,
+    factor_hbm,
     mask,
     ancestor,
     out,
     gathered,
+    factor,
     turned,
     tiles,
     parts,
@@ -104,6 +106,7 @@
     plane_sems,
     line_sems,
     shared_sems,
+    small_loads,
 ):
     n_rows = lax.axis_size("prow")
     n_cols = lax.axis_size("pcol")
@@ -129,14 +132,19 @@
     upper, lower = pl.ds(0, half), pl.ds(half, half)
     group = 2 * n_rows
     member = row * 2 + core
-    height = width // group
+    height = 3 * width // (2 * group)
 
     def load(t):
         start = pl.multiple_of(chunk_of(order[t % 4], deep) * slab + (t // 4) * LANES, LANES)
         return pltpu.make_async_copy(ancestor.at[:, pl.ds(start, LANES)], tiles.at[t], loads.at[t])
 
-    for t in range(4 * lanes_each):
+    def load_factor(k):
+        return pltpu.make_async_copy(factor_hbm.at[k], factor.at[k], small_loads.at[k])
+
+    load_factor(0).start()
+    for t in range(AHEAD):
         load(t).start()
+    blocks_here = rows_here // WIDTH
 
     def in_plane(d):
         peer = lax.rem(member + d, group)
@@ -156,9 +164,12 @@
         pl.semaphore_signal(barrier, inc=1, device_id=origin, device_id_type=MESH)
 
     def turn(k):
-        for i in range(0, rows_here, WIDTH):
-            block = factor[k, pl.ds(i, WIDTH)].T.astype(jnp.float32) * mask[pl.ds(k, 1), pl.ds(i, WIDTH)]
-            turned[pl.ds(k * width, width), pl.ds(i, WIDTH)] = block.astype(jnp.bfloat16)
+        load_factor(k).wait()
+        for i in range(blocks_here):
+            at = pl.ds(i * WIDTH, WIDTH)
+            kept = mask[k, row * blocks_here + i].astype(jnp.float32)
+            block = factor[k, at].T.astype(jnp.float32) * kept
+            turned[pl.ds(k * width, width), at] = block.astype(jnp.bfloat16)
 
     turn(0)
 
@@ -185,6 +196,11 @@
             t = 4 * j + q
             if k == 0:
                 load(t).wait()
+                if t + AHEAD < 4 * lanes_each:
+                    load(t + AHEAD).start()
+                if t == 2:
+                    for other in range(1, count):
+                        load_factor(other).start()
             value = tiles[t]
             high = value.astype(jnp.bfloat16)
             low = (value - high.astype(jnp.float32)).astype(jnp.bfloat16)
@@ -243,7 +259,10 @@
                 (((1,), (1,)), ((), ())),
                 preferred_element_type=jnp.float32,
             )
-        term[k] = total
+        mid = width // 2
+        term[k, pl.ds(0, mid)] = total[:mid, :mid]
+        term[k, pl.ds(mid, mid)] = total[:mid, mid:]
+        term[k, pl.ds(2 * mid, mid)] = total[mid:, mid:]
         copies = []
         for d in range(1, group):
             peer, device = in_plane(d)
@@ -282,37 +301,44 @@
         for copy in copies:
             copy.wait_recv()
         for d in range(group):
-            gathered[pl.ds(k * width + d * height, height)] = decode(shared.at[k, d])
+            term[k, pl.ds(d * height, height)] = decode(shared.at[k, d])
+        cross = term[k, pl.ds(mid, mid)]
+        top = jnp.concatenate([term[k, pl.ds(0, mid)], cross], axis=1)
+        bottom = jnp.concatenate([cross.T, term[k, pl.ds(2 * mid, mid)]], axis=1)
+        gathered[k] = jnp.concatenate([top, bottom], axis=0)
         for copy in sent + copies:
             copy.wait_send()
 
     def turn_back(k):
         for j in range(lanes_each):
-            out[k, pl.ds(j * LANES, LANES)] = parts[4 * (k * lanes_each + j)].T
-
-    compute(0)
-    for k in range(1, count):
-        turn(k)
-    for i in range(1, pieces):
+            start = row * rows_here + column * slab + j * LANES
+            kept = mask[k, lax.div(start, WIDTH)].astype(jnp.float32)
+            out[k, pl.ds(j * LANES, LANES)] = parts[4 * (k * lanes_each + j)].T * kept
+
+    for i in range(pieces):
         compute(i)
-        forward(i - 1)
+        if i == 0:
+            for k in range(1, count):
+                turn(k)
+        if i >= 1:
+            forward(i - 1)
         if i >= 2:
             end(i - 2)
     forward(pieces - 1)
+    end(pieces - 2)
     running = [diagonal(k) for k in range(count)]
-    for k in range(count - 1):
-        next(running[k])
-    end(pieces - 2)
     for k in range(count - 1):
         next(running[k])
     end(pieces - 1)
     for k in range(count - 1):
         next(running[k])
+    next(running[count - 1])
+    for k in range(count - 1):
+        next(running[k])
         turn_back(k)
     next(running[count - 1])
     turn_back(count - 1)
-    for _ in range(2):
-        next(running[count - 1])
+    next(running[count - 1])
     for k in range(count):
         next(running[k], None)
     for i in range(pieces):
@@ -334,18 +360,19 @@
     pieces = count * lanes_each
     half = width // 2
     group, n_deep = 2 * n_rows, n_cols // 2
-    height = width // group
-    vmem = pl.BlockSpec(memory_space=pltpu.VMEM)
+    height = 3 * width // (2 * group)
+    vmem, hbm = pl.BlockSpec(memory_space=pltpu.VMEM), pl.BlockSpec(memory_space=pl.ANY)
     f32, i16 = jnp.float32, jnp.int16
     return pl.pallas_call(
         fused_kernel,
         out_shape=(
             jax.ShapeDtypeStruct((count, slab, width), f32),
-            jax.ShapeDtypeStruct((count * width, width), f32),
+            jax.ShapeDtypeStruct((count, width, width), f32),
         ),
-        in_specs=[vmem, vmem, pl.BlockSpec(memory_space=pl.ANY)],
+        in_specs=[hbm, pl.BlockSpec(memory_space=pltpu.SMEM), hbm],
         out_specs=(vmem, vmem),
         scratch_shapes=[
+            pltpu.VMEM(factor.shape, factor.dtype),
             pltpu.VMEM((count * width, depth), jnp.bfloat16),
             pltpu.VMEM((4 * lanes_each, depth, LANES), f32),
             pltpu.VMEM((4 * pieces, width, LANES), f32),
@@ -355,19 +382,20 @@
             pltpu.VMEM((pieces, 2, half, LANES), i16),
             pltpu.VMEM((pieces, width, LANES), i16),
             pltpu.VMEM((pieces, width, LANES), i16),
-            pltpu.VMEM((count, width, width), f32),
-            pltpu.VMEM((count, group - 1, height, width), i16),
-            pltpu.VMEM((count, group - 1, height, width), i16),
-            pltpu.VMEM((count, n_deep, height, width), i16),
-            pltpu.VMEM((count, group, height, width), i16),
+            pltpu.VMEM((count, group * height, width // 2), f32),
+            pltpu.VMEM((count, group - 1, height, width // 2), i16),
+            pltpu.VMEM((count, group - 1, height, width // 2), i16),
+            pltpu.VMEM((count, n_deep, height, width // 2), i16),
+            pltpu.VMEM((count, group, height, width // 2), i16),
             pltpu.SemaphoreType.DMA((4 * lanes_each,)),
             pltpu.SemaphoreType.DMA((2, pieces, 7)),
             pltpu.SemaphoreType.DMA((2, count, group - 1)),
             pltpu.SemaphoreType.DMA((2, count, n_deep - 1)),
             pltpu.SemaphoreType.DMA((2, count, group - 1)),
+            pltpu.SemaphoreType.DMA((count,)),
         ],
         compiler_params=pltpu.CompilerParams(
-            collective_id=1, has_side_effects=True, vmem_limit_bytes=56 * 1024 * 1024
+            collective_id=1, has_side_effects=True, vmem_limit_bytes=50 * 1024 * 1024
         ),
     )(factor, mask, ancestor)
 
@@ -390,15 +418,15 @@
     column = lax.axis_index("pcol")
     grid_row = lax.axis_index("prow")
     slab = rows_here // n_cols
+    fits = n_rows == 4 and n_cols % 2 == 0 and n_cols > 2 and width == WIDTH
+    fits = fits and slab % LANES == 0 and slab * n_rows == ancestor.shape[1]
+    if fits:
+        placed, total = fused(factor, block_mask, ancestor)
+        return (-placed, inverse_diag.astype(jnp.float32) + total)
     row_mask = jnp.repeat(block_mask, WIDTH, axis=1).astype(jnp.float32)
     own_mask = lax.dynamic_slice_in_dim(row_mask, grid_row * rows_here, rows_here, 1)
     slab_mask = lax.dynamic_slice_in_dim(own_mask, column * slab, slab, 1)
     inverse = inverse_diag.astype(jnp.float32)
-    fits = n_rows == 4 and n_cols % 2 == 0 and n_cols > 2 and width == WIDTH
-    fits = fits and slab % LANES == 0 and slab * n_rows == ancestor.shape[1]
-    if fits:
-        placed, total = fused(factor, own_mask, ancestor)
-        return (-slab_mask[:, :, None] * placed, inverse + total.reshape(inverse.shape))
     masked = factor * own_mask[:, :, None].astype(factor.dtype)
     turned = masked.transpose(0, 2, 1).reshape(count * width, rows_here)
     placed = product_plain(turned, ancestor).reshape(count, width, slab)

time: 57.5 us -> 49.3 us (0.86)
  Pallas kernels: 51 us -> 46.1 us
  other arithmetic: 4.87 us -> 1.78 us
    pallas_call x1, Pallas kernels: 51 us -> 46.1 us  [fused(): pl.pallas_call(fused_kernel, out_shape=(jax.ShapeDtypeStruct((count, slab...]
    mul x1 -> x0, other arithmetic: 2.18 us -> none  [shards(): -slab_mask[:, :, None] * placed]
    add x1, other arithmetic: 1.89 us -> 0.85 us  [shards(): return (-placed, inverse_diag.astype(jnp.float32) + total)]
    neg x1, other arithmetic: 0.08 us -> 0.93 us  [shards(): return (-placed, inverse_diag.astype(jnp.float32) + total)]
    convert_element_type x1 -> x0, other arithmetic: 0.72 us -> none  [shards(): row_mask = jnp.repeat(block_mask, WIDTH, axis=1).astype(jnp.float32)]
    dynamic_slice x1 -> x0, local copies, waits for them, and re-layouts: 0.61 us -> none  [shards(): lax.dynamic_slice_in_dim(row_mask, grid_row * rows_here, rows_here, 1)]
where the time goes in v3:
time: 49.3 us; the launch traced here: 49.2 us
  Pallas kernels  46.1 us (94%)
  other arithmetic  1.78 us (4%)
  local copies, waits for them, and re-layouts  0.68 us (1%)
  between operations  0.65 us (1%)
    pallas_call x1, Pallas kernels, fused(): pl.pallas_call(fused_kernel, out_shape=(jax.ShapeDtypeStruct((count, slab...  46.1 us

profile of v3, /device:TPU:0, one launch (start us, length us, event | category | flops | bytes accessed | tf_op | source)
XLA Modules:
  0.0 49.2 jit_solution(6469603212917485073)
XLA Ops:
  0.6 0.0 copy-start
  0.6 0.7 %copy-done = s32[2,48]{1,0:T(2,128)S(1)} copy-done((s32[2,48]{1,0:T(2,128)S(1)}, s32[2,48]{1,0:T(2,128)}, u32[]{:S(2)}) %copy-start) | copy-done | bytes 408
  1.3 0.0 copy-start.1
  1.3 46.1 %shard_map.59 = (f32[2,384,256]{2,1,0:T(8,128)S(1)}, f32[2,256,256]{2,1,0:T(8,128)S(1)}) custom-call(bf16[2,3072,256]{2,1,0:T(8,128)(2,1)} %factor_hbm.1, s32[2,48]{1,0:T(2,128)S(1)} %copy-done, f32[3072,1536]{1,0:T(8,128)} %ancestor.1), custom_call_target="tpu_custom_call" | custom-call | tf_op jit(solution)/shard_map/pallas_call | solution.py:366
  47.4 0.9 %neg.3 = f32[2,384,256]{2,1,0:T(8,128)} negate(f32[2,384,256]{2,1,0:T(8,128)S(1)} %get-tuple-element.4) | non-fusion elementwise | flops 196608 | bytes 1572864 | tf_op jit(solution)/shard_map/neg | solution.py:425
  48.3 0.0 copy-done.1
  48.3 0.8 %convert_add_fusion = f32[2,256,256]{2,1,0:T(8,128)} fusion(f32[2,256,256]{2,1,0:T(8,128)S(1)} %get-tuple-element.5, bf16[2,256,256]{2,1,0:T(8,128)(2,1)S(1)} %copy-done.1), kind=kLoop, calls=%fused_computation | loop fusion | flops 262144 | bytes 1310720 | tf_op jit(solution)/shard_map/add | solution.py:425
Async XLA Ops:
  0.6 0.7 %copy-start = (s32[2,48]{1,0:T(2,128)S(1)}, s32[2,48]{1,0:T(2,128)}, u32[]{:S(2)}) copy-start(s32[2,48]{1,0:T(2,128)} %mask.1) | copy-start | bytes 1156
  1.3 47.0 %copy-start.1 = (bf16[2,256,256]{2,1,0:T(8,128)(2,1)S(1)}, bf16[2,256,256]{2,1,0:T(8,128)(2,1)}, u32[]{:S(2)}) copy-start(bf16[2,256,256]{2,1,0:T(8,128)(2,1)} %param.6) | copy-start | bytes 786436

commit v4 on v3

--- a/solution.py
+++ b/solution.py
@@ -66,7 +66,7 @@
 
 
 LANES = 128
-AHEAD = 3
+AHEAD = 4
 
 
 def remote(source, target, sems, piece, number, device):
@@ -144,6 +144,8 @@
     load_factor(0).start()
     for t in range(AHEAD):
         load(t).start()
+    for other in range(1, count):
+        load_factor(other).start()
     blocks_here = rows_here // WIDTH
 
     def in_plane(d):
@@ -198,9 +200,6 @@
                 load(t).wait()
                 if t + AHEAD < 4 * lanes_each:
                     load(t + AHEAD).start()
-                if t == 2:
-                    for other in range(1, count):
-                        load_factor(other).start()
             value = tiles[t]
             high = value.astype(jnp.bfloat16)
             low = (value - high.astype(jnp.float32)).astype(jnp.bfloat16)
@@ -208,16 +207,18 @@
             for h in range(2):
                 both = dot(turned[pl.ds(k * width + h * half, half)], stacked)
                 parts[4 * i + q, pl.ds(h * half, half)] = both[:, :LANES] + both[:, LANES:]
-            for s in ((0, 2), (1,), (3,), ())[q]:
+            ready = ((0, 2), (1,), (3,), ())[q]
+            for s in ready:
                 encode(parts[4 * i + q, (upper, upper, lower, lower)[s]], first_out.at[i, s])
+            for s in ready:
                 early(i, s).start()
 
     def forward(i):
         early(i, 0).wait_recv()
+        early(i, 2).wait_recv()
         encode(parts[4 * i + 2, upper] + decode(first.at[i, 0]), second_out.at[i, 0])
+        encode(parts[4 * i + 1, lower] + decode(first.at[i, 2]), second_out.at[i, 1])
         late(i, 0).start()
-        early(i, 2).wait_recv()
-        encode(parts[4 * i + 1, lower] + decode(first.at[i, 2]), second_out.at[i, 1])
         late(i, 1).start()
 
     def end(i):
@@ -264,16 +265,18 @@
         term[k, pl.ds(mid, mid)] = total[:mid, mid:]
         term[k, pl.ds(2 * mid, mid)] = total[mid:, mid:]
         copies = []
+        for d in range(group):
+            encode(term[k, pl.ds(d * height, height)], plane_out.at[k, d])
         for d in range(1, group):
             peer, device = in_plane(d)
-            encode(term[k, pl.ds(pl.multiple_of(peer * height, height), height)], plane_out.at[k, d - 1])
-            copy = remote(plane_out.at[k, d - 1], plane.at[k, d - 1], plane_sems, k, d - 1, device)
+            copy = remote(plane_out.at[k, peer], plane.at[k, d - 1], plane_sems, k, d - 1, device)
             copy.start()
             copies.append(copy)
         yield
+        for copy in copies:
+            copy.wait_recv()
         total = term[k, pl.ds(pl.multiple_of(member * height, height), height)]
         for d in range(1, group):
-            copies[d - 1].wait_recv()
             total = total + decode(plane.at[k, d - 1])
         encode(total, line.at[k, deep])
         sent = copies
@@ -327,18 +330,12 @@
     forward(pieces - 1)
     end(pieces - 2)
     running = [diagonal(k) for k in range(count)]
-    for k in range(count - 1):
-        next(running[k])
     end(pieces - 1)
-    for k in range(count - 1):
-        next(running[k])
-    next(running[count - 1])
-    for k in range(count - 1):
-        next(running[k])
+    for _ in range(3):
+        for k in range(count):
+            next(running[k])
+    for k in range(count):
         turn_back(k)
-    next(running[count - 1])
-    turn_back(count - 1)
-    next(running[count - 1])
     for k in range(count):
         next(running[k], None)
     for i in range(pieces):
@@ -383,7 +380,7 @@
             pltpu.VMEM((pieces, width, LANES), i16),
             pltpu.VMEM((pieces, width, LANES), i16),
             pltpu.VMEM((count, group * height, width // 2), f32),
-            pltpu.VMEM((count, group - 1, height, width // 2), i16),
+            pltpu.VMEM((count, group, height, width // 2), i16),
             pltpu.VMEM((count, group - 1, height, width // 2), i16),
             pltpu.VMEM((count, n_deep, height, width // 2), i16),
             pltpu.VMEM((count, group, height, width // 2), i16),

time: 49.3 us -> 47.9 us (0.972)
  Pallas kernels: 46.1 us -> 44.6 us
    pallas_call x1, Pallas kernels: 46.1 us -> 44.6 us  [fused(): pl.pallas_call(fused_kernel, out_shape=(jax.ShapeDtypeStruct((count, slab...]
where the time goes in v4:
time: 47.9 us; the launch traced here: 47.7 us
  Pallas kernels  44.6 us (93%)
  other arithmetic  1.78 us (4%)
  local copies, waits for them, and re-layouts  0.68 us (1%)
  between operations  0.65 us (1%)
    pallas_call x1, Pallas kernels, fused(): pl.pallas_call(fused_kernel, out_shape=(jax.ShapeDtypeStruct((count, slab...  44.6 us

profile of v4, /device:TPU:0, one launch (start us, length us, event | category | flops | bytes accessed | tf_op | source)
XLA Modules:
  0.0 47.7 jit_solution(12706123223185228654)
XLA Ops:
  0.6 0.0 copy-start
  0.6 0.7 %copy-done = s32[2,48]{1,0:T(2,128)S(1)} copy-done((s32[2,48]{1,0:T(2,128)S(1)}, s32[2,48]{1,0:T(2,128)}, u32[]{:S(2)}) %copy-start) | copy-done | bytes 408
  1.3 0.0 copy-start.1
  1.3 44.6 %shard_map.59 = (f32[2,384,256]{2,1,0:T(8,128)S(1)}, f32[2,256,256]{2,1,0:T(8,128)S(1)}) custom-call(bf16[2,3072,256]{2,1,0:T(8,128)(2,1)} %factor_hbm.1, s32[2,48]{1,0:T(2,128)S(1)} %copy-done, f32[3072,1536]{1,0:T(8,128)} %ancestor.1), custom_call_target="tpu_custom_call" | custom-call | tf_op jit(solution)/shard_map/pallas_call | solution.py:363
  45.9 0.9 %neg.3 = f32[2,384,256]{2,1,0:T(8,128)} negate(f32[2,384,256]{2,1,0:T(8,128)S(1)} %get-tuple-element.4) | non-fusion elementwise | flops 196608 | bytes 1572864 | tf_op jit(solution)/shard_map/neg | solution.py:422
  46.9 0.0 copy-done.1
  46.9 0.8 %convert_add_fusion = f32[2,256,256]{2,1,0:T(8,128)} fusion(f32[2,256,256]{2,1,0:T(8,128)S(1)} %get-tuple-element.5, bf16[2,256,256]{2,1,0:T(8,128)(2,1)S(1)} %copy-done.1), kind=kLoop, calls=%fused_computation | loop fusion | flops 262144 | bytes 1310720 | tf_op jit(solution)/shard_map/add | solution.py:422
Async XLA Ops:
  0.6 0.7 %copy-start = (s32[2,48]{1,0:T(2,128)S(1)}, s32[2,48]{1,0:T(2,128)}, u32[]{:S(2)}) copy-start(s32[2,48]{1,0:T(2,128)} %mask.1) | copy-start | bytes 1156
  1.3 45.5 %copy-start.1 = (bf16[2,256,256]{2,1,0:T(8,128)(2,1)S(1)}, bf16[2,256,256]{2,1,0:T(8,128)(2,1)}, u32[]{:S(2)}) copy-start(bf16[2,256,256]{2,1,0:T(8,128)(2,1)} %param.6) | copy-start | bytes 786436

commit v5 on v4

--- a/solution.py
+++ b/solution.py
@@ -320,13 +320,13 @@
 
     for i in range(pieces):
         compute(i)
-        if i == 0:
-            for k in range(1, count):
-                turn(k)
         if i >= 1:
             forward(i - 1)
         if i >= 2:
             end(i - 2)
+        if i == lanes_each - 1:
+            for k in range(1, count):
+                turn(k)
     forward(pieces - 1)
     end(pieces - 2)
     running = [diagonal(k) for k in range(count)]

time: 47.9 us -> 47.4 us (0.990)
  Pallas kernels: 44.6 us -> 44.1 us
    pallas_call x1, Pallas kernels: 44.6 us -> 44.1 us  [fused(): pl.pallas_call(fused_kernel, out_shape=(jax.ShapeDtypeStruct((count, slab...]
where the time goes in v5:
time: 47.4 us; the launch traced here: 47.2 us
  Pallas kernels  44.1 us (93%)
  other arithmetic  1.78 us (4%)
  local copies, waits for them, and re-layouts  0.68 us (1%)
  between operations  0.65 us (1%)
    pallas_call x1, Pallas kernels, fused(): pl.pallas_call(fused_kernel, out_shape=(jax.ShapeDtypeStruct((count, slab...  44.1 us

profile of v5, /device:TPU:0, one launch (start us, length us, event | category | flops | bytes accessed | tf_op | source)
XLA Modules:
  0.0 47.2 jit_solution(15734748710452398718)
XLA Ops:
  0.6 0.0 copy-start
  0.6 0.7 %copy-done = s32[2,48]{1,0:T(2,128)S(1)} copy-done((s32[2,48]{1,0:T(2,128)S(1)}, s32[2,48]{1,0:T(2,128)}, u32[]{:S(2)}) %copy-start) | copy-done | bytes 408
  1.3 0.0 copy-start.1
  1.3 44.1 %shard_map.59 = (f32[2,384,256]{2,1,0:T(8,128)S(1)}, f32[2,256,256]{2,1,0:T(8,128)S(1)}) custom-call(bf16[2,3072,256]{2,1,0:T(8,128)(2,1)} %factor_hbm.1, s32[2,48]{1,0:T(2,128)S(1)} %copy-done, f32[3072,1536]{1,0:T(8,128)} %ancestor.1), custom_call_target="tpu_custom_call" | custom-call | tf_op jit(solution)/shard_map/pallas_call | solution.py:363
  45.4 0.9 %neg.3 = f32[2,384,256]{2,1,0:T(8,128)} negate(f32[2,384,256]{2,1,0:T(8,128)S(1)} %get-tuple-element.4) | non-fusion elementwise | flops 196608 | bytes 1572864 | tf_op jit(solution)/shard_map/neg | solution.py:422
  46.4 0.0 copy-done.1
  46.4 0.8 %convert_add_fusion = f32[2,256,256]{2,1,0:T(8,128)} fusion(f32[2,256,256]{2,1,0:T(8,128)S(1)} %get-tuple-element.5, bf16[2,256,256]{2,1,0:T(8,128)(2,1)S(1)} %copy-done.1), kind=kLoop, calls=%fused_computation | loop fusion | flops 262144 | bytes 1310720 | tf_op jit(solution)/shard_map/add | solution.py:422
Async XLA Ops:
  0.6 0.7 %copy-start = (s32[2,48]{1,0:T(2,128)S(1)}, s32[2,48]{1,0:T(2,128)}, u32[]{:S(2)}) copy-start(s32[2,48]{1,0:T(2,128)} %mask.1) | copy-start | bytes 1156
  1.3 45.0 %copy-start.1 = (bf16[2,256,256]{2,1,0:T(8,128)(2,1)S(1)}, bf16[2,256,256]{2,1,0:T(8,128)(2,1)}, u32[]{:S(2)}) copy-start(bf16[2,256,256]{2,1,0:T(8,128)(2,1)} %param.6) | copy-start | bytes 786436
